TPU v7x, 32 devices: a whole 2x2x4 slice. The times are simulated.
32 devices in a mesh: row: 8 (over y, x, core), col: 4 (over z).
Axes of the slice: x: 2, y: 2, z: 4, core: 2. Of those that a mesh axis runs over, the one named last changes fastest.
Arguments:
- start_modes: float32 [32, 131072], P(None, ('row', 'col')), may hold values from -6 to 6
- energies: float32 [131072], P(('row', 'col')), may hold values from -0.5 to 0.5
- coupling: float32 [2048, 20, 4096], P('row', 'col'), may hold values from -0.078125 to 0.078125
- pattern: int32 [2048, 20], P('row', 'col'), may hold values from 0 to 2047, as said below
Outputs:
- filtered: float32 [32, 131072], P(None, ('row', 'col'))
- previous: float32 [32, 131072], P(None, ('row', 'col'))
Inputs may be any that keep to these rules, and one draw needn't show every extreme that they name: In block row i, the 5 entries pattern[i, c * 5] to pattern[i, c * 5 + 4] are distinct block columns j with (j // 64) % 4 == c.
All inputs are finite; a program needn't handle non-finite values.
Results may differ from a plain program's by a relative error of at most 0.0001.
Values sent between devices are 32-bit elements; how exact they have to be, the bound alone decides.
A program may use at most 192 MiB of HBM per device.

v0:
```python
import jax
import jax.numpy as jnp
from jax import lax
from jax.sharding import PartitionSpec as P

BLOCK = 64
DEGREE = 3


def shards(start_modes, energies, coupling, pattern):
    col_count = lax.axis_size("col")
    mode_count, piece_len = start_modes.shape
    per_piece = piece_len // BLOCK
    rows_here, slot_count = pattern.shape
    piece_ids = pattern // per_piece
    places = piece_ids // col_count * per_piece + pattern % per_piece
    block_mats = coupling.reshape(rows_here, slot_count, BLOCK, BLOCK)

    def coupled(gathered, row_count):
        blocks = gathered.reshape(mode_count, -1, BLOCK)
        sub_mats = block_mats
        picked = jnp.take(blocks, places.reshape(-1), axis=1).reshape(
            mode_count, row_count, per_piece, slot_count, BLOCK
        )
        sub_mats = sub_mats.reshape(row_count, per_piece, slot_count, BLOCK, BLOCK)
        result = jnp.einsum("mqksb,qksab->qmka", picked, sub_mats, precision=lax.Precision.HIGHEST)
        return result.reshape(row_count, mode_count, per_piece * BLOCK)

    def operate(vector):
        gathered = lax.all_gather(vector, "row", axis=1, tiled=True)
        shares_row = lax.psum_scatter(
            coupled(gathered, col_count), "col", scatter_dimension=0, tiled=True
        )[0]
        return energies[None, :] * vector + shares_row

    previous = start_modes
    current = operate(start_modes)
    for degree in range(DEGREE - 1):
        upcoming = 2.0 * operate(current) - previous
        previous = current
        current = upcoming
    return (current, previous)


def solution(mesh):
    in_specs = (P(None, ("row", "col")), P(("row", "col")), P("row", "col", None), P("row", "col"))
    out_specs = (P(None, ("row", "col")), P(None, ("row", "col")))
    return jax.shard_map(shards, mesh=mesh, in_specs=in_specs, out_specs=out_specs, check_vma=False)
```

profile of v0, /device:TPU:0, one launch (start us, length us, event | category | flops | bytes accessed | tf_op | source)
XLA Modules:
  0.0 585.6 jit_solution(14820434715844887029)
XLA Ops:
  7.2 0.0 all-gather.4.cloned.1.call-start
  7.2 0.7 all-gather.4.cloned.1.call-update
  7.9 0.0 reduce-scatter.4.cloned.1.call-start
  7.9 0.7 fusion.21
  8.7 0.1 copy.12
  8.8 0.2 reshape.43
  9.0 33.5 %reshape_reshape.2 = f32[4,64,5,64,64]{4,3,1,0,2:T(8,128)} reshape(f32[256,5,4096]{2,0,1:T(8,128)} %param.8) | data formatting | bytes 41943040 | tf_op jit(solution)/shard_map/reshape;reshape | solution.py:25
  42.5 6.7 %all-gather.4.cloned.1.call-done = f32[32,32768]{1,0:T(8,128)} async-done(((f32[32,4096]{1,0:T(8,128)}), f32[32,32768]{1,0:T(8,128)}) %all-gather.4.cloned.1.call-update) | async-done | bytes 4194320 | tf_op jit(solution)/shard_map/all_gather | solution.py:30
  49.2 7.3 %reshape.42 = f32[32,512,64]{2,1,0:T(8,128)} reshape(f32[32,32768]{1,0:T(8,128)} %all-gather.4.cloned.1.call-done) | data formatting | bytes 8388608 | tf_op jit(solution)/shard_map/reshape | solution.py:20
  56.5 11.5 %copy.13 = f32[32,512,64]{2,0,1:T(8,128)} copy(f32[32,512,64]{2,1,0:T(8,128)} %reshape.42) | data formatting | bytes 8388608 | tf_op jit(solution)/shard_map/reshape | solution.py:20
  68.0 13.0 %gather_fusion = f32[1280,32,64]{2,1,0:T(8,128)} fusion(f32[32,512,64]{2,0,1:T(8,128)} %copy.13, s32[2048]{0:T(1024)S(1)} %pad_clamp_fusion), kind=kCustom, calls=%fused_computation.clone | custom fusion | bytes 20976640 | tf_op jit(solution)/shard_map/jit(_take)/gather | solution.py:22
  81.0 17.1 %broadcast_select_fusion.2 = f32[1280,32,64]{2,1,0:T(8,128)} fusion(f32[1280,32,64]{2,1,0:T(8,128)} %gather_fusion, pred[1280]{0:T(1024)(128)(4,1)S(1)} %compare_and_fusion), kind=kLoop, calls=%fused_computation.11 | loop fusion | flops 2621440 | bytes 20972800 | tf_op jit(solution)/shard_map/jit(_take)/select_n | solution.py:22
  98.1 48.6 %fusion.6 = f32[4,32,64,64]{3,1,2,0:T(8,128)S(1)} fusion(f32[32,4,64,5,64]{4,0,3,2,1:T(8,128)} %bitcast.50, f32[4,64,5,64,64]{4,3,1,0,2:T(8,128)} %reshape_reshape.2), kind=kOutput, calls=%fused_computation.12 | convolution fusion | flops 2013265920 | bytes 33554432 | tf_op jit(solution)/shard_map/mqksb,qksab->qmka/dot_general | solution.py:26
  146.7 4.4 copy.15
  151.1 4.8 reshape.45
  155.8 0.0 reduce-scatter.4.cloned.1.call-update
  155.9 0.0 all-gather.6.cloned.1.call-start
  155.9 43.7 %reduce-scatter.4.cloned.1.call-done = f32[1,32,4096]{2,1,0:T(8,128)} async-done(((f32[4,32,4096]{2,1,0:T(8,128)}), f32[1,32,4096]{2,1,0:T(8,128)}) %reduce-scatter.4.cloned.1.call-update) | async-done | bytes 524304 | tf_op jit(solution)/shard_map/reduce_scatter | solution.py:31
  199.7 1.9 bitcast_add_fusion.2
  201.6 0.0 all-gather.6.cloned.1.call-update
  201.6 0.0 reduce-scatter.6.cloned.1.call-start
  201.6 36.3 %all-gather.6.cloned.1.call-done = f32[32,32768]{1,0:T(8,128)} async-done(((f32[32,4096]{1,0:T(8,128)}), f32[32,32768]{1,0:T(8,128)}) %all-gather.6.cloned.1.call-update) | async-done | bytes 4194320 | tf_op jit(solution)/shard_map/all_gather | solution.py:30
  238.0 7.3 %reshape.46 = f32[32,512,64]{2,1,0:T(8,128)} reshape(f32[32,32768]{1,0:T(8,128)} %all-gather.6.cloned.1.call-done) | data formatting | bytes 8388608 | tf_op jit(solution)/shard_map/reshape | solution.py:20
  245.3 11.5 %copy.16 = f32[32,512,64]{2,0,1:T(8,128)} copy(f32[32,512,64]{2,1,0:T(8,128)} %reshape.46) | data formatting | bytes 8388608 | tf_op jit(solution)/shard_map/reshape | solution.py:20
  256.8 13.0 %gather_fusion.1 = f32[1280,32,64]{2,1,0:T(8,128)} fusion(f32[32,512,64]{2,0,1:T(8,128)} %copy.16, s32[2048]{0:T(1024)S(1)} %pad_clamp_fusion), kind=kCustom, calls=%fused_computation.1.clone | custom fusion | bytes 20976640 | tf_op jit(solution)/shard_map/jit(_take)/gather | solution.py:22
  269.7 17.1 %broadcast_select_fusion.1 = f32[1280,32,64]{2,1,0:T(8,128)} fusion(f32[1280,32,64]{2,1,0:T(8,128)} %gather_fusion.1, pred[1280]{0:T(1024)(128)(4,1)S(1)} %compare_and_fusion), kind=kLoop, calls=%fused_computation.10 | loop fusion | flops 2621440 | bytes 20972800 | tf_op jit(solution)/shard_map/jit(_take)/select_n | solution.py:22
  286.8 48.5 %fusion.9 = f32[4,32,64,64]{3,1,2,0:T(8,128)S(1)} fusion(f32[32,4,64,5,64]{4,0,3,2,1:T(8,128)} %bitcast.51, f32[4,64,5,64,64]{4,3,1,0,2:T(8,128)} %reshape_reshape.2), kind=kOutput, calls=%fused_computation.13 | convolution fusion | flops 2013265920 | bytes 33554432 | tf_op jit(solution)/shard_map/mqksb,qksab->qmka/dot_general | solution.py:26
  335.4 4.4 copy.18
  339.7 4.8 reshape.48
  344.5 0.0 reduce-scatter.6.cloned.1.call-update
  344.5 0.0 all-gather.8.cloned.1.call-start
  344.6 43.7 %reduce-scatter.6.cloned.1.call-done = f32[1,32,4096]{2,1,0:T(8,128)} async-done(((f32[4,32,4096]{2,1,0:T(8,128)}), f32[1,32,4096]{2,1,0:T(8,128)}) %reduce-scatter.6.cloned.1.call-update) | async-done | bytes 524304 | tf_op jit(solution)/shard_map/reduce_scatter | solution.py:31
  388.3 0.0 copy-done
  388.3 1.9 fusion.18
  390.3 0.0 all-gather.8.cloned.1.call-update
  390.3 0.0 reduce-scatter.8.cloned.1.call-start
  390.3 36.1 %all-gather.8.cloned.1.call-done = f32[32,32768]{1,0:T(8,128)} async-done(((f32[32,4096]{1,0:T(8,128)}), f32[32,32768]{1,0:T(8,128)}) %all-gather.8.cloned.1.call-update) | async-done | bytes 4194320 | tf_op jit(solution)/shard_map/all_gather | solution.py:30
  426.5 7.3 %reshape.49 = f32[32,512,64]{2,1,0:T(8,128)} reshape(f32[32,32768]{1,0:T(8,128)} %all-gather.8.cloned.1.call-done) | data formatting | bytes 8388608 | tf_op jit(solution)/shard_map/reshape | solution.py:20
  433.8 11.5 %copy.19 = f32[32,512,64]{2,0,1:T(8,128)} copy(f32[32,512,64]{2,1,0:T(8,128)} %reshape.49) | data formatting | bytes 8388608 | tf_op jit(solution)/shard_map/reshape | solution.py:20
  445.2 13.0 %gather_fusion.2 = f32[1280,32,64]{2,1,0:T(8,128)} fusion(f32[32,512,64]{2,0,1:T(8,128)} %copy.19, s32[2048]{0:T(1024)S(1)} %pad_clamp_fusion), kind=kCustom, calls=%fused_computation.2.clone | custom fusion | bytes 20976640 | tf_op jit(solution)/shard_map/jit(_take)/gather | solution.py:22
  458.2 17.1 %broadcast_select_fusion = f32[1280,32,64]{2,1,0:T(8,128)} fusion(f32[1280,32,64]{2,1,0:T(8,128)} %gather_fusion.2, pred[1280]{0:T(1024)(128)(4,1)S(1)} %compare_and_fusion), kind=kLoop, calls=%fused_computation.9 | loop fusion | flops 2621440 | bytes 20972800 | tf_op jit(solution)/shard_map/jit(_take)/select_n | solution.py:22
  475.3 48.3 %fusion.12 = f32[4,32,64,64]{3,1,2,0:T(8,128)S(1)} fusion(f32[32,4,64,5,64]{4,0,3,2,1:T(8,128)} %bitcast.49, f32[4,64,5,64,64]{4,3,1,0,2:T(8,128)} %reshape_reshape.2), kind=kOutput, calls=%fused_computation.14 | convolution fusion | flops 2013265920 | bytes 33554432 | tf_op jit(solution)/shard_map/mqksb,qksab->qmka/dot_general | solution.py:26
  523.6 4.4 copy.21
  528.0 4.8 reshape.51
  532.8 0.0 reduce-scatter.8.cloned.1.call-update
  532.8 43.8 %reduce-scatter.8.cloned.1.call-done = f32[1,32,4096]{2,1,0:T(8,128)} async-done(((f32[4,32,4096]{2,1,0:T(8,128)}), f32[1,32,4096]{2,1,0:T(8,128)}) %reduce-scatter.8.cloned.1.call-update) | async-done | bytes 524304 | tf_op jit(solution)/shard_map/reduce_scatter | solution.py:31
  576.6 0.0 copy-done.2
  576.6 1.9 fusion.16
  (9 shorter events, 0.0 us)
Async XLA Ops:
  7.2 42.1 %all-gather.4.cloned.1.call-start = ((), (), s32[]{:S(2)}) async-start(), calls=%async_computation.3 | async-start | bytes 4718592 | tf_op jit(solution)/shard_map/all_gather | solution.py:30
  7.9 191.8 %reduce-scatter.4.cloned.1.call-start = ((), (), s32[]{:S(2)}) async-start(), calls=%async_computation.4 | async-start | bytes 2621440 | tf_op jit(solution)/shard_map/reduce_scatter | solution.py:31
  98.1 101.6 %copy-start.1 = (f32[32,4096]{1,0:T(8,128)S(1)}, f32[32,4096]{1,0:T(8,128)}, u32[]{:S(2)}) copy-start(f32[32,4096]{1,0:T(8,128)} %param.6) | copy-start | bytes 1572868
  98.1 101.6 %copy-start.3 = (f32[4096]{0:T(1024)S(1)}, f32[4096]{0:T(1024)}, u32[]{:S(2)}) copy-start(f32[4096]{0:T(1024)} %param.7) | copy-start | bytes 49156
  155.9 82.1 %all-gather.6.cloned.1.call-start = ((), (), s32[]{:S(2)}) async-start(), calls=%async_computation.5 | async-start | bytes 4718592 | tf_op jit(solution)/shard_map/all_gather | solution.py:30
  201.6 186.7 %reduce-scatter.6.cloned.1.call-start = ((), (), s32[]{:S(2)}) async-start(), calls=%async_computation.6 | async-start | bytes 2621440 | tf_op jit(solution)/shard_map/reduce_scatter | solution.py:31
  286.8 101.5 %copy-start = (f32[32,4096]{1,0:T(8,128)S(1)}, f32[32,4096]{1,0:T(8,128)}, u32[]{:S(2)}) copy-start(f32[32,4096]{1,0:T(8,128)} %bitcast_add_fusion.2) | copy-start | bytes 1572868
  344.5 81.9 %all-gather.8.cloned.1.call-start = ((), (), s32[]{:S(2)}) async-start(), calls=%async_computation.7 | async-start | bytes 4718592 | tf_op jit(solution)/shard_map/all_gather | solution.py:30
  390.3 186.3 %reduce-scatter.8.cloned.1.call-start = ((), (), s32[]{:S(2)}) async-start(), calls=%async_computation.8 | async-start | bytes 2621440 | tf_op jit(solution)/shard_map/reduce_scatter | solution.py:31
  475.3 101.3 %copy-start.2 = (f32[32,4096]{1,0:T(8,128)S(1)}, f32[32,4096]{1,0:T(8,128)}, u32[]{:S(2)}) copy-start(f32[32,4096]{1,0:T(8,128)} %fusion.18) | copy-start | bytes 1572868
Sparse Core Ops, SparseCore 0:
  9.9 39.2 all-gather.3
  156.0 43.6 reduce-scatter.3
  202.1 35.7 all-gather.5
  344.6 43.6 reduce-scatter.5
  390.6 35.7 all-gather.7
  532.9 43.6 reduce-scatter.7
where the time goes:
time: 595 us; the launch traced here: 586 us
  waiting for transfers between devices  211 us (35%)
  local copies, waits for them, and re-layouts  157 us (26%)
  matrix products  145 us (24%)
  other arithmetic  57.8 us (10%)
  between operations  14.4 us (2%)
    dot_general x3, matrix products, coupled(): jnp.einsum('mqksb,qksab->qmka', picked, sub_mats, precision=lax.Precision...  145 us
    reduce_scatter x3, waiting for transfers between devices, operate(): lax.psum_scatter(coupled(gathered, col_count), 'col', scatter_dimension=0...  131 us
    all_gather x3, waiting for transfers between devices, operate(): gathered = lax.all_gather(vector, 'row', axis=1, tiled=True)  79.1 us
    reshape x6, local copies, waits for them, and re-layouts, coupled(): blocks = gathered.reshape(mode_count, -1, BLOCK)  56.4 us
    select_n x4, other arithmetic, coupled(): jnp.take(blocks, places.reshape(-1), axis=1)  51.3 us
    gather x3, local copies, waits for them, and re-layouts, coupled(): jnp.take(blocks, places.reshape(-1), axis=1)  39 us
    another operation x1, local copies, waits for them, and re-layouts, coupled(): sub_mats = sub_mats.reshape(row_count, per_piece, slot_count, BLOCK, BLOCK)  33.5 us
    reshape x3, local copies, waits for them, and re-layouts, coupled(): return result.reshape(row_count, mode_count, per_piece * BLOCK)  14.3 us
  transfers between devices with their start and end apart: 6, of which 6 were waited for; matrix products, arithmetic and copies ran while one was open for 6% of the time, Pallas kernels for 0%

commit v1 on v0

v1 whole, which is shorter than its diff:
```python
import functools

import jax
import jax.numpy as jnp
from jax import lax
from jax.experimental import pallas as pl
from jax.experimental.pallas import tpu as pltpu
from jax.sharding import PartitionSpec as P

BLOCK = 64
DEGREE = 3
LANES = 128


def low_half(shape):
    return lax.broadcasted_iota(jnp.int32, shape, len(shape) - 1) < BLOCK


def split(x):
    high = x.astype(jnp.bfloat16)
    return high, (x - high.astype(jnp.float32)).astype(jnp.bfloat16)


def prepare_kernel(slots, c_ref, out_ref, stage):
    pairs = (slots + 1) // 2
    group = c_ref.shape[1]
    low = low_half((group, LANES))
    for k in range(pairs):
        for p in range(BLOCK // 2):
            first = c_ref[2 * k, :, p * LANES : (p + 1) * LANES]
            first_turned = pltpu.roll(first, BLOCK, 1)
            if 2 * k + 1 < slots:
                second = c_ref[2 * k + 1, :, p * LANES : (p + 1) * LANES]
                second_turned = pltpu.roll(second, BLOCK, 1)
            else:
                second = second_turned = jnp.zeros_like(first)
            stage[k, pl.ds(2 * p, group, stride=BLOCK), :] = jnp.where(low, first, second_turned)
            stage[k, pl.ds(2 * p + 1, group, stride=BLOCK), :] = jnp.where(low, first_turned, second)
    for k in range(pairs):
        for i in range(group):
            high, rest = split(stage[k, i * BLOCK : (i + 1) * BLOCK, :])
            out_ref[i, :BLOCK, k * LANES : (k + 1) * LANES] = high
            out_ref[i, BLOCK:, k * LANES : (k + 1) * LANES] = rest


def prepare(coupling):
    rows, slots, entries = coupling.shape
    group = 8
    pairs = (slots + 1) // 2
    return pl.pallas_call(
        functools.partial(prepare_kernel, slots),
        grid=(rows // group,),
        in_specs=[pl.BlockSpec((slots, group, entries), lambda g: (0, g, 0))],
        out_specs=pl.BlockSpec((group, 2 * BLOCK, pairs * LANES), lambda g: (g, 0, 0)),
        out_shape=jax.ShapeDtypeStruct((rows, 2 * BLOCK, pairs * LANES), jnp.bfloat16),
        scratch_shapes=[pltpu.VMEM((pairs, group * BLOCK, LANES), jnp.float32)],
        cost_estimate=pl.CostEstimate(flops=10 * coupling.size, bytes_accessed=9 * coupling.size, transcendentals=0),
        name="prepare",
    )(jnp.transpose(coupling, (1, 0, 2)))


def fill_blocks(gathered_ref, blocks, pieces, modes, tiles):
    low = low_half((modes, LANES))

    def piece(index, carry):
        for t in range(tiles):
            x = gathered_ref[index, :, t * LANES : (t + 1) * LANES]
            turned = pltpu.roll(x, BLOCK, 1)
            for side, value in enumerate((jnp.where(low, x, turned), jnp.where(low, turned, x))):
                high, rest = split(value)
                place = index * (2 * tiles) + 2 * t + side
                blocks[place, :modes, :] = high
                blocks[place, modes:, :] = rest
        return carry

    lax.fori_loop(0, pieces, piece, 0)


def couple_kernel(slots, places_ref, gathered_ref, c_ref, out_ref, blocks):
    step = pl.program_id(0)
    group = c_ref.shape[0]
    pieces, modes, piece_len = gathered_ref.shape

    @pl.when(step == 0)
    def _():
        fill_blocks(gathered_ref, blocks, pieces, modes, piece_len // LANES)

    low = low_half((2 * modes, LANES))
    low_out = low_half((modes, LANES))
    done = []
    for i in range(group):
        base = (step * group + i) * slots
        picked = [blocks[places_ref[base + s]] for s in range(slots)]
        sides = [
            jnp.where(low, picked[2 * k], picked[2 * k + 1]) if 2 * k + 1 < slots else picked[2 * k]
            for k in range((slots + 1) // 2)
        ]
        product = lax.dot_general(
            jnp.concatenate(sides, axis=1), c_ref[i], (((1,), (1,)), ((), ())), preferred_element_type=jnp.float32
        )
        total = product[:modes] + product[modes:]
        done.append(total + pltpu.roll(total, BLOCK, 1))
        if i % 2 == 1:
            out_ref[0, :, (i // 2) * LANES : (i // 2 + 1) * LANES] = jnp.where(low_out, done[i - 1], done[i])


def couple(gathered, places, prepared, slots, col_count):
    pieces, modes, piece_len = gathered.shape
    rows = prepared.shape[0]
    per_piece = piece_len // BLOCK
    group = min(16, per_piece)
    per_part = per_piece // group
    return pl.pallas_call(
        functools.partial(couple_kernel, slots),
        grid_spec=pltpu.PrefetchScalarGridSpec(
            num_scalar_prefetch=1,
            grid=(rows // group,),
            in_specs=[
                pl.BlockSpec(gathered.shape, lambda g, *_: (0, 0, 0), pipeline_mode=pl.Buffered(1)),
                pl.BlockSpec((group,) + prepared.shape[1:], lambda g, *_: (g, 0, 0)),
            ],
            out_specs=pl.BlockSpec((1, modes, group * BLOCK), lambda g, *_: (g // per_part, 0, g % per_part)),
            scratch_shapes=[pltpu.VMEM((pieces * per_piece, 2 * modes, LANES), jnp.bfloat16)],
        ),
        out_shape=jax.ShapeDtypeStruct((col_count, modes, piece_len), jnp.float32),
        cost_estimate=pl.CostEstimate(
            flops=4 * modes * prepared.size, bytes_accessed=2 * prepared.size + 8 * gathered.size, transcendentals=0
        ),
        name="couple",
    )(places, gathered, prepared)


def shards(start_modes, energies, coupling, pattern):
    col_count = lax.axis_size("col")
    piece_len = start_modes.shape[1]
    per_piece = piece_len // BLOCK
    slots = pattern.shape[1]
    places = (pattern // per_piece // col_count * per_piece + pattern % per_piece).reshape(-1)
    prepared = prepare(coupling)

    def operate(vector):
        gathered = lax.all_gather(vector, "row", axis=0, tiled=False)
        shares = couple(gathered, places, prepared, slots, col_count)
        share = lax.psum_scatter(shares, "col", scatter_dimension=0, tiled=True)[0]
        return energies[None, :] * vector + share

    previous = start_modes
    current = operate(start_modes)
    for degree in range(DEGREE - 1):
        upcoming = 2.0 * operate(current) - previous
        previous = current
        current = upcoming
    return (current, previous)


def solution(mesh):
    in_specs = (P(None, ("row", "col")), P(("row", "col")), P("row", "col", None), P("row", "col"))
    out_specs = (P(None, ("row", "col")), P(None, ("row", "col")))
    return jax.shard_map(shards, mesh=mesh, in_specs=in_specs, out_specs=out_specs, check_vma=False)
```

time: 595 us -> 342 us (0.57); the launches traced: 586 us -> 340 us
  local copies, waits for them, and re-layouts: 157 us -> 0.95 us
  matrix products: 145 us -> 0 us
  Pallas kernels: 0 us -> 109 us
  other arithmetic: 57.8 us -> 6.44 us
    dot_general x3 -> x0, matrix products: 145 us -> none  [coupled(): jnp.einsum('mqksb,qksab->qmka', picked, sub_mats, precision=lax.Precision...]
    pallas_call x0 -> x4, Pallas kernels: none -> 109 us  [the longest x3 74.2 us: couple(): pl.pallas_call(functools.partial(couple_kernel, slots), grid_spec=pltpu.P...]
    reshape x10 -> x1, local copies, waits for them, and re-layouts: 70.8 us -> 0.8 us  [shards(): (pattern // per_piece // col_count * per_piece + pattern % per_piece).res...]
    select_n x4 -> x0, other arithmetic: 51.3 us -> none  [coupled(): jnp.take(blocks, places.reshape(-1), axis=1)]
    gather x3 -> x0, local copies, waits for them, and re-layouts: 39 us -> none  [coupled(): jnp.take(blocks, places.reshape(-1), axis=1)]
    another operation x1 -> x0, local copies, waits for them, and re-layouts: 33.5 us -> none  [coupled(): sub_mats = sub_mats.reshape(row_count, per_piece, slot_count, BLOCK, BLOCK)]
    transpose x3 -> x0, local copies, waits for them, and re-layouts: 13.1 us -> none  [coupled(): jnp.einsum('mqksb,qksab->qmka', picked, sub_mats, precision=lax.Precision...]
  transfers between devices with their start and end apart: 6 -> 6, of which waited for: 6 -> 6; matrix products, arithmetic and copies ran while one was open for 6% -> 0% of each run, Pallas kernels for 0% -> 10%
where the time goes in v1:
time: 342 us; the launch traced here: 340 us
  waiting for transfers between devices  209 us (61%)
  Pallas kernels  109 us (32%)
  between operations  14.1 us (4%)
  other arithmetic  6.44 us (2%)
    reduce_scatter x3, waiting for transfers between devices, operate(): share = lax.psum_scatter(shares, 'col', scatter_dimension=0, tiled=True)[0]  131 us
    all_gather x3, waiting for transfers between devices, operate(): gathered = lax.all_gather(vector, 'row', axis=0, tiled=False)  76.7 us
    pallas_call x3, Pallas kernels, couple(): pl.pallas_call(functools.partial(couple_kernel, slots), grid_spec=pltpu.P...  74.2 us
    pallas_call x1, Pallas kernels, prepare(): pl.pallas_call(functools.partial(prepare_kernel, slots), grid=(rows // gr...  35.3 us
  transfers between devices with their start and end apart: 6, of which 6 were waited for; matrix products, arithmetic and copies ran while one was open for 0% of the time, Pallas kernels for 10%

profile of v1, /device:TPU:0, one launch (start us, length us, event | category | flops | bytes accessed | tf_op | source)
XLA Modules:
  0.0 340.0 jit_solution(1208670210053753784)
XLA Ops:
  7.2 0.0 all-gather.7.cloned.1.call-start
  7.2 0.7 all-gather.7.cloned.1.call-update
  7.9 0.0 reduce-scatter.4.cloned.1.call-start
  7.9 0.7 fusion.6
  8.7 0.1 copy.6
  8.8 0.8 reshape.8.places_ref
  9.6 35.3 %prepare.1.c_ref = bf16[256,128,384]{2,1,0:T(8,128)(2,1)} custom-call(f32[5,256,4096]{2,1,0:T(8,128)} %bitcast.18), custom_call_target="tpu_custom_call" | custom-call | flops 52428800 | bytes 47185920 | tf_op jit(solution)/shard_map/prepare/pallas_call | solution.py:50
  44.9 4.3 %all-gather.7.cloned.1.call-done = f32[256,4096]{1,0:T(8,128)} async-done(((f32[32,4096]{1,0:T(8,128)}), f32[256,4096]{1,0:T(8,128)}) %all-gather.7.cloned.1.call-update) | async-done | bytes 4194320 | tf_op jit(solution)/shard_map/all_gather | solution.py:142
  49.2 0.0 copy-start.1
  49.2 0.0 copy-start.3
  49.2 24.7 %couple.3 = f32[4,32,4096]{2,1,0:T(8,128)} custom-call(s32[1280]{0:T(1024)} %reshape.8.places_ref, f32[8,32,4096]{2,1,0:T(8,128)} %bitcast.19, bf16[256,128,384]{2,1,0:T(8,128)(2,1)} %prepare.1.c_ref), custom_call_target="tpu_custom_call" | custom-call | flops 1610612736 | bytes 33554432 | tf_op jit(solution)/shard_map/couple/pallas_call | solution.py:113
  73.9 0.0 reduce-scatter.4.cloned.1.call-update
  73.9 0.0 all-gather.9.cloned.1.call-start
  74.0 43.7 %reduce-scatter.4.cloned.1.call-done = f32[1,32,4096]{2,1,0:T(8,128)} async-done(((f32[4,32,4096]{2,1,0:T(8,128)}), f32[1,32,4096]{2,1,0:T(8,128)}) %reduce-scatter.4.cloned.1.call-update) | async-done | bytes 524304 | tf_op jit(solution)/shard_map/reduce_scatter | solution.py:144
  117.7 0.0 copy-done.1
  117.7 0.0 copy-done.3
  117.7 1.9 bitcast_add_fusion.2
  119.6 0.0 all-gather.9.cloned.1.call-update
  119.7 0.0 reduce-scatter.6.cloned.1.call-start
  119.7 36.3 %all-gather.9.cloned.1.call-done = f32[256,4096]{1,0:T(8,128)} async-done(((f32[32,4096]{1,0:T(8,128)}), f32[256,4096]{1,0:T(8,128)}) %all-gather.9.cloned.1.call-update) | async-done | bytes 4194320 | tf_op jit(solution)/shard_map/all_gather | solution.py:142
  156.0 0.0 copy-start
  156.0 24.7 %couple.4 = f32[4,32,4096]{2,1,0:T(8,128)} custom-call(s32[1280]{0:T(1024)} %reshape.8.places_ref, f32[8,32,4096]{2,1,0:T(8,128)} %bitcast.21, bf16[256,128,384]{2,1,0:T(8,128)(2,1)} %prepare.1.c_ref), custom_call_target="tpu_custom_call" | custom-call | flops 1610612736 | bytes 33554432 | tf_op jit(solution)/shard_map/couple/pallas_call | solution.py:113
  180.8 0.0 reduce-scatter.6.cloned.1.call-update
  180.8 0.0 all-gather.11.cloned.1.call-start
  180.8 43.7 %reduce-scatter.6.cloned.1.call-done = f32[1,32,4096]{2,1,0:T(8,128)} async-done(((f32[4,32,4096]{2,1,0:T(8,128)}), f32[1,32,4096]{2,1,0:T(8,128)}) %reduce-scatter.6.cloned.1.call-update) | async-done | bytes 524304 | tf_op jit(solution)/shard_map/reduce_scatter | solution.py:144
  224.6 0.0 copy-done
  224.6 1.9 fusion.3
  226.5 0.0 all-gather.11.cloned.1.call-update
  226.5 0.0 reduce-scatter.8.cloned.1.call-start
  226.6 36.1 %all-gather.11.cloned.1.call-done = f32[256,4096]{1,0:T(8,128)} async-done(((f32[32,4096]{1,0:T(8,128)}), f32[256,4096]{1,0:T(8,128)}) %all-gather.11.cloned.1.call-update) | async-done | bytes 4194320 | tf_op jit(solution)/shard_map/all_gather | solution.py:142
  262.7 0.0 copy-start.2
  262.7 24.7 %couple.5 = f32[4,32,4096]{2,1,0:T(8,128)} custom-call(s32[1280]{0:T(1024)} %reshape.8.places_ref, f32[8,32,4096]{2,1,0:T(8,128)} %bitcast.20, bf16[256,128,384]{2,1,0:T(8,128)(2,1)} %prepare.1.c_ref), custom_call_target="tpu_custom_call" | custom-call | flops 1610612736 | bytes 33554432 | tf_op jit(solution)/shard_map/couple/pallas_call | solution.py:113
  287.4 0.0 reduce-scatter.8.cloned.1.call-update
  287.4 43.8 %reduce-scatter.8.cloned.1.call-done = f32[1,32,4096]{2,1,0:T(8,128)} async-done(((f32[4,32,4096]{2,1,0:T(8,128)}), f32[1,32,4096]{2,1,0:T(8,128)}) %reduce-scatter.8.cloned.1.call-update) | async-done | bytes 524304 | tf_op jit(solution)/shard_map/reduce_scatter | solution.py:144
  331.2 0.0 copy-done.2
  331.2 1.9 fusion.1
Async XLA Ops:
  7.2 42.0 %all-gather.7.cloned.1.call-start = ((), (), s32[]{:S(2)}) async-start(), calls=%async_computation.6 | async-start | bytes 4718592 | tf_op jit(solution)/shard_map/all_gather | solution.py:142
  7.9 109.8 %reduce-scatter.4.cloned.1.call-start = ((), (), s32[]{:S(2)}) async-start(), calls=%async_computation.3 | async-start | bytes 2621440 | tf_op jit(solution)/shard_map/reduce_scatter | solution.py:144
  49.2 68.5 %copy-start.1 = (f32[32,4096]{1,0:T(8,128)S(1)}, f32[32,4096]{1,0:T(8,128)}, u32[]{:S(2)}) copy-start(f32[32,4096]{1,0:T(8,128)} %param.4) | copy-start | bytes 1572868
  49.2 68.5 %copy-start.3 = (f32[4096]{0:T(1024)S(1)}, f32[4096]{0:T(1024)}, u32[]{:S(2)}) copy-start(f32[4096]{0:T(1024)} %param.5) | copy-start | bytes 49156
  73.9 82.1 %all-gather.9.cloned.1.call-start = ((), (), s32[]{:S(2)}) async-start(), calls=%async_computation.7 | async-start | bytes 4718592 | tf_op jit(solution)/shard_map/all_gather | solution.py:142
  119.7 104.9 %reduce-scatter.6.cloned.1.call-start = ((), (), s32[]{:S(2)}) async-start(), calls=%async_computation.4 | async-start | bytes 2621440 | tf_op jit(solution)/shard_map/reduce_scatter | solution.py:144
  156.0 68.5 %copy-start = (f32[32,4096]{1,0:T(8,128)S(1)}, f32[32,4096]{1,0:T(8,128)}, u32[]{:S(2)}) copy-start(f32[32,4096]{1,0:T(8,128)} %bitcast_add_fusion.2) | copy-start | bytes 1572868
  180.8 81.9 %all-gather.11.cloned.1.call-start = ((), (), s32[]{:S(2)}) async-start(), calls=%async_computation.8 | async-start | bytes 4718592 | tf_op jit(solution)/shard_map/all_gather | solution.py:142
  226.5 104.7 %reduce-scatter.8.cloned.1.call-start = ((), (), s32[]{:S(2)}) async-start(), calls=%async_computation.5 | async-start | bytes 2621440 | tf_op jit(solution)/shard_map/reduce_scatter | solution.py:144
  262.7 68.5 %copy-start.2 = (f32[32,4096]{1,0:T(8,128)S(1)}, f32[32,4096]{1,0:T(8,128)}, u32[]{:S(2)}) copy-start(f32[32,4096]{1,0:T(8,128)} %fusion.3) | copy-start | bytes 1572868
Sparse Core Ops, SparseCore 0:
  9.9 39.2 all-gather.6
  74.1 43.6 reduce-scatter.3
  120.2 35.7 all-gather.8
  180.9 43.6 reduce-scatter.5
  226.9 35.7 all-gather.10
  287.6 43.6 reduce-scatter.7

commit v2 on v0

v2 whole, which is shorter than its diff:
```python
import functools

import jax
import jax.numpy as jnp
from jax import lax
from jax.experimental import pallas as pl
from jax.experimental.pallas import tpu as pltpu
from jax.sharding import PartitionSpec as P

BLOCK = 64
DEGREE = 3
LANES = 128


def low_half(shape):
    return lax.broadcasted_iota(jnp.int32, shape, len(shape) - 1) < BLOCK


def split(x):
    high = x.astype(jnp.bfloat16)
    return high, (x - high.astype(jnp.float32)).astype(jnp.bfloat16)


MESH = pl.DeviceIdType.MESH


def filter_kernel(
    slots, n_row, n_col, halves,
    places_ref, start_ref, energies_ref, coupling_ref, filtered_ref, previous_ref,
    c_buf, stage, prepared, gathered, blocks, first_ref, partial, landed,
    c_sem, gather_send, gather_recv, share_send, share_recv,
):
    row, col = lax.axis_index("row"), lax.axis_index("col")
    chips = n_row // 2
    chip, core = row // 2, row % 2
    partner = chip * 2 + (1 - core)
    modes, piece_len = start_ref.shape
    part = modes // halves
    tiles = piece_len // LANES
    per_piece = piece_len // BLOCK
    rows = prepared.shape[0]
    group = min(16, per_piece)
    terms = (start_ref, first_ref, previous_ref, filtered_ref)

    def same_core(d):
        return (chip + d) % chips * 2 + core

    def other_core(d):
        return (chip + d) % chips * 2 + (1 - core)

    def share_of(k, h):
        return terms[k].at[pl.ds(h * part, part), :]

    barrier = pltpu.get_barrier_semaphore()
    for d in range(1, chips):
        pl.semaphore_signal(barrier, inc=1, device_id=(same_core(d), col), device_id_type=MESH)
    pl.semaphore_signal(barrier, inc=1, device_id=(partner, col), device_id_type=MESH)
    for d in range(1, n_col):
        pl.semaphore_signal(barrier, inc=1, device_id=(row, (col + d) % n_col), device_id_type=MESH)
    pl.semaphore_wait(barrier, chips + n_col - 1)

    def gather_copy(k, h, source, slot, sem, target):
        return pltpu.make_async_remote_copy(
            src_ref=source,
            dst_ref=gathered.at[k, h, slot],
            send_sem=gather_send.at[k, h, sem],
            recv_sem=gather_recv.at[k, h, slot],
            device_id=(target, col),
            device_id_type=MESH,
        )

    def own_copies(k, h):
        source = share_of(k, h)
        return [gather_copy(k, h, source, row, d, same_core(d)) for d in range(1, chips)] + [
            gather_copy(k, h, source, row, 0, partner)
        ]

    def passed_copies(k, h):
        return [
            gather_copy(k, h, gathered.at[k, h, same_core(-d)], same_core(-d), chips + d, partner)
            for d in range(1, chips)
        ]

    def arrival(k, h, slot):
        return gather_copy(k, h, gathered.at[k, h, slot], slot, 0, partner)

    def gather_start(k, h):
        for copy in own_copies(k, h):
            copy.start()
        gathered[k, h, row] = share_of(k, h)[...]

    def gather_finish(k, h):
        for d, copy in enumerate(passed_copies(k, h), 1):
            arrival(k, h, same_core(-d)).wait_recv()
            copy.start()
        arrival(k, h, partner).wait_recv()
        for d in range(1, chips):
            arrival(k, h, other_core(-d)).wait_recv()

    def share_copy(k, h, target):
        return pltpu.make_async_remote_copy(
            src_ref=partial.at[k, h, target],
            dst_ref=landed.at[k, h, col],
            send_sem=share_send.at[k, h, target],
            recv_sem=share_recv.at[k, h, col],
            device_id=(row, target),
            device_id_type=MESH,
        )

    def share_arrival(k, h, origin):
        return pltpu.make_async_remote_copy(
            src_ref=partial.at[k, h, origin],
            dst_ref=landed.at[k, h, origin],
            send_sem=share_send.at[k, h, origin],
            recv_sem=share_recv.at[k, h, origin],
            device_id=(row, origin),
            device_id_type=MESH,
        )

    def compute(k, h):
        low = low_half((part, LANES))
        low_picked = low_half((2 * part, LANES))

        def fill(index, carry):
            for t in range(tiles):
                x = gathered[k, h, index, :, t * LANES : (t + 1) * LANES]
                turned = pltpu.roll(x, BLOCK, 1)
                for side, value in enumerate((jnp.where(low, x, turned), jnp.where(low, turned, x))):
                    high, rest = split(value)
                    place = index * (2 * tiles) + 2 * t + side
                    blocks[place, :part, :] = high
                    blocks[place, part:, :] = rest
            return carry

        lax.fori_loop(0, n_row, fill, 0)

        def one_part(d, carry):
            target = (col + d) % n_col

            def some_rows(step, carry):
                first = target * per_piece + step * group
                done = []
                for i in range(group):
                    base = (first + i) * slots
                    picked = [blocks[places_ref[base + s]] for s in range(slots)]
                    sides = [
                        jnp.where(low_picked, picked[2 * q], picked[2 * q + 1]) if 2 * q + 1 < slots else picked[2 * q]
                        for q in range((slots + 1) // 2)
                    ]
                    product = lax.dot_general(
                        jnp.concatenate(sides, axis=1),
                        prepared[first + i],
                        (((1,), (1,)), ((), ())),
                        preferred_element_type=jnp.float32,
                    )
                    total = product[:part] + product[part:]
                    done.append(total + pltpu.roll(total, BLOCK, 1))
                width = group * BLOCK
                wide = [jnp.where(low, done[2 * q], done[2 * q + 1]) for q in range(group // 2)]
                partial[k, h, target, :, pl.ds(pl.multiple_of(step * width, width), width)] = jnp.concatenate(wide, axis=1)
                return carry

            lax.fori_loop(0, per_piece // group, some_rows, 0)
            return carry

        def one_sent(d, carry):
            one_part(d, carry)
            share_copy(k, h, (col + d) % n_col).start()
            return carry

        lax.fori_loop(1, n_col, one_sent, 0)
        one_part(0, 0)

    def update(k, h):
        for d in range(1, n_col):
            share_arrival(k, h, (col + d) % n_col).wait_recv()
        here = slice(h * part, (h + 1) * part)

        def tile(t, carry):
            at = pl.ds(pl.multiple_of(t * LANES, LANES), LANES)
            total = partial[k, h, col, :, at]
            for d in range(1, n_col):
                total = total + landed[k, h, (col + d) % n_col, :, at]
            total = energies_ref[:, at] * terms[k][here, at] + total
            if k > 0:
                total = 2.0 * total - terms[k - 1][here, at]
            terms[k + 1][here, at] = total
            return carry

        lax.fori_loop(0, tiles, tile, 0)

    for h in range(halves):
        gather_start(0, h)

    chunk = c_buf.shape[2]
    chunks = rows // chunk

    def fetch(index, slot):
        return pltpu.make_async_copy(
            coupling_ref.at[:, pl.ds(pl.multiple_of(index * chunk, chunk), chunk), :], c_buf.at[slot], c_sem.at[slot]
        )

    fetch(0, 0).start()

    def prepare_chunk(index, carry):
        slot = index % 2

        @pl.when(index + 1 < chunks)
        def _():
            fetch(index + 1, 1 - slot).start()

        fetch(index, slot).wait()
        pairs = (slots + 1) // 2
        low = low_half((chunk, LANES))
        for q in range(pairs):
            for p in range(BLOCK // 2):
                lane = slice(p * LANES, (p + 1) * LANES)
                one = c_buf[slot, 2 * q, :, lane]
                one_turned = pltpu.roll(one, BLOCK, 1)
                if 2 * q + 1 < slots:
                    two = c_buf[slot, 2 * q + 1, :, lane]
                    two_turned = pltpu.roll(two, BLOCK, 1)
                else:
                    two = two_turned = jnp.zeros_like(one)
                stage[q, pl.ds(2 * p, chunk, stride=BLOCK), :] = jnp.where(low, one, two_turned)
                stage[q, pl.ds(2 * p + 1, chunk, stride=BLOCK), :] = jnp.where(low, one_turned, two)
        for q in range(pairs):
            for i in range(chunk):
                high, rest = split(stage[q, i * BLOCK : (i + 1) * BLOCK, :])
                prepared[index * chunk + i, :BLOCK, q * LANES : (q + 1) * LANES] = high
                prepared[index * chunk + i, BLOCK:, q * LANES : (q + 1) * LANES] = rest
        return carry

    lax.fori_loop(0, chunks, prepare_chunk, 0)

    for k in range(DEGREE):
        for h in range(halves):
            if k > 0:
                update(k - 1, h)
                gather_start(k, h)
            gather_finish(k, h)
            compute(k, h)
    for h in range(halves):
        update(DEGREE - 1, h)
    for k in range(DEGREE):
        for h in range(halves):
            for copy in own_copies(k, h) + passed_copies(k, h):
                copy.wait_send()
            for d in range(1, n_col):
                share_copy(k, h, (col + d) % n_col).wait_send()


def shards(start_modes, energies, coupling, pattern):
    n_row, n_col = lax.axis_size("row"), lax.axis_size("col")
    modes, piece_len = start_modes.shape
    per_piece = piece_len // BLOCK
    rows, slots, entries = coupling.shape
    pairs = (slots + 1) // 2
    chunk, halves = 8, 2
    part = modes // halves
    places = (pattern // per_piece // n_col * per_piece + pattern % per_piece).reshape(-1)
    vmem = pl.BlockSpec(memory_space=pltpu.VMEM)
    filtered, previous = pl.pallas_call(
        functools.partial(filter_kernel, slots, n_row, n_col, halves),
        in_specs=[pl.BlockSpec(memory_space=pltpu.SMEM), vmem, vmem, pl.BlockSpec(memory_space=pl.ANY)],
        out_specs=[vmem, vmem],
        out_shape=[jax.ShapeDtypeStruct(start_modes.shape, jnp.float32)] * 2,
        scratch_shapes=[
            pltpu.VMEM((2, slots, chunk, entries), jnp.float32),
            pltpu.VMEM((pairs, chunk * BLOCK, LANES), jnp.float32),
            pltpu.VMEM((rows, 2 * BLOCK, pairs * LANES), jnp.bfloat16),
            pltpu.VMEM((DEGREE, halves, n_row, part, piece_len), jnp.float32),
            pltpu.VMEM((n_row * per_piece, 2 * part, LANES), jnp.bfloat16),
            pltpu.VMEM((modes, piece_len), jnp.float32),
            pltpu.VMEM((DEGREE, halves, n_col, part, piece_len), jnp.float32),
            pltpu.VMEM((DEGREE, halves, n_col, part, piece_len), jnp.float32),
            pltpu.SemaphoreType.DMA((2,)),
            pltpu.SemaphoreType.DMA((DEGREE, halves, n_row)),
            pltpu.SemaphoreType.DMA((DEGREE, halves, n_row)),
            pltpu.SemaphoreType.DMA((DEGREE, halves, n_col)),
            pltpu.SemaphoreType.DMA((DEGREE, halves, n_col)),
        ],
        compiler_params=pltpu.CompilerParams(collective_id=0, has_side_effects=True, vmem_limit_bytes=67043328),
        name="filter",
    )(places, start_modes, energies.reshape(1, -1), jnp.transpose(coupling, (1, 0, 2)))
    return filtered, previous


def solution(mesh):
    in_specs = (P(None, ("row", "col")), P(("row", "col")), P("row", "col", None), P("row", "col"))
    out_specs = (P(None, ("row", "col")), P(None, ("row", "col")))
    return jax.shard_map(shards, mesh=mesh, in_specs=in_specs, out_specs=out_specs, check_vma=False)
```

time: 595 us -> 208 us (0.35); the launches traced: 586 us -> 206 us
  waiting for transfers between devices: 211 us -> 0 us
  Pallas kernels: 0 us -> 200 us
  local copies, waits for them, and re-layouts: 157 us -> 4.68 us
  matrix products: 145 us -> 0 us
  other arithmetic: 57.8 us -> 0.72 us
  between operations: 14.4 us -> 0.65 us
    pallas_call x0 -> x1, Pallas kernels: none -> 200 us  [shards(): pl.pallas_call(functools.partial(filter_kernel, slots, n_row, n_col, halv...]
    dot_general x3 -> x0, matrix products: 145 us -> none  [coupled(): jnp.einsum('mqksb,qksab->qmka', picked, sub_mats, precision=lax.Precision...]
    reduce_scatter x3 -> x0, waiting for transfers between devices: 131 us -> none  [operate(): lax.psum_scatter(coupled(gathered, col_count), 'col', scatter_dimension=0...]
    all_gather x3 -> x0, waiting for transfers between devices: 79.1 us -> none  [operate(): gathered = lax.all_gather(vector, 'row', axis=1, tiled=True)]
    reshape x10 -> x1, local copies, waits for them, and re-layouts: 70.8 us -> 0.81 us  [shards(): (pattern // per_piece // n_col * per_piece + pattern % per_piece).reshape...]
    select_n x4 -> x0, other arithmetic: 51.3 us -> none  [coupled(): jnp.take(blocks, places.reshape(-1), axis=1)]
    gather x3 -> x0, local copies, waits for them, and re-layouts: 39 us -> none  [coupled(): jnp.take(blocks, places.reshape(-1), axis=1)]
    another operation x1 -> x0, local copies, waits for them, and re-layouts: 33.5 us -> none  [coupled(): sub_mats = sub_mats.reshape(row_count, per_piece, slot_count, BLOCK, BLOCK)]
  transfers between devices with their start and end apart: 6 -> 0, of which waited for: 6 -> 0; matrix products, arithmetic and copies ran while one was open for 6% -> 0% of each run, Pallas kernels for 0% -> 0%
where the time goes in v2:
time: 208 us; the launch traced here: 206 us
  Pallas kernels  200 us (96%)
  local copies, waits for them, and re-layouts  4.68 us (2%)
    pallas_call x1, Pallas kernels, shards(): pl.pallas_call(functools.partial(filter_kernel, slots, n_row, n_col, halv...  200 us

profile of v2, /device:TPU:0, one launch (start us, length us, event | category | flops | bytes accessed | tf_op | source)
XLA Modules:
  0.0 205.9 jit_solution(8549986431815910680)
XLA Ops:
  0.6 0.7 fusion.2
  1.3 0.1 copy.6
  1.5 0.8 reshape.10.places_ref
  2.3 199.8 %filter.1 = (f32[32,4096]{1,0:T(8,128)}, f32[32,4096]{1,0:T(8,128)}) custom-call(s32[1280]{0:T(1024)} %reshape.10.places_ref, f32[32,4096]{1,0:T(8,128)} %start_ref.1, f32[1,4096]{1,0:T(1,128)} %bitcast.3, f32[5,256,4096]{2,1,0:T(8,128)} %bitcast.2), custom_call_target="tpu_custom_call" | custom-call | tf_op jit(solution)/shard_map/filter/pallas_call | solution.py:263
  202.2 1.9 copy.9
  204.0 1.9 copy.10
